TPU v7x, 32 devices: a whole 2x2x4 slice. The times are simulated.
32 devices in a mesh: dp: 16 (over z, y, x), tensor: 2 (over core).
Axes of the slice: x: 2, y: 2, z: 4, core: 2. Of those that a mesh axis runs over, the one named last changes fastest.
Arguments:
- tokens: bfloat16 [32768, 768], P('dp'), may hold values from -6 to 6
- cotangent: bfloat16 [32768, 768], P('dp'), may hold values from -6 to 6
- seq_ids: int32 [32768], P('dp'), may hold values from 0 to 39, as said below
- block_slot: int32 [216], replicated, may hold values from 0 to 223, as said below
- masters: float32 [2, 224, 128, 128], P('tensor', 'dp')
- left_stats: float32 [2, 224, 128, 128], P('tensor', 'dp'), as said below
- right_stats: float32 [2, 224, 128, 128], P('tensor', 'dp'), as said below
- left_roots: float32 [2, 224, 128, 128], P('tensor', 'dp'), as said below
- right_roots: float32 [2, 224, 128, 128], P('tensor', 'dp'), as said below
- vectors: float32 [9984], replicated
- vector_momentum: float32 [9984], replicated, may hold values from -0.9 to 0.9
Outputs:
- mixed: bfloat16 [32768, 768], P(('dp', 'tensor'))
- input_grad: float32 [32768, 768], P(('dp', 'tensor'))
- matrix_grads: float32 [2, 224, 128, 128], P('tensor', 'dp')
- new_masters: float32 [2, 224, 128, 128], P('tensor', 'dp')
- new_left: float32 [2, 224, 128, 128], P('tensor', 'dp')
- new_right: float32 [2, 224, 128, 128], P('tensor', 'dp')
- new_vectors: float32 [9984], replicated
- new_vector_momentum: float32 [9984], replicated
Inputs may be any that keep to these rules, and one draw needn't show every extreme that they name: `seq_ids`: each aligned block of 2048 tokens holds either one sequence or 4 sequences of 512 tokens, half of the blocks of each kind; ids count the sequences in order from 0 and are equal within a sequence. `block_slot`: Distinct; slot s belongs to index s // 14 of dp; slots that no block names hold no block. `left_stats`: symmetric in each slot. `right_stats`: symmetric in each slot. `left_roots`: symmetric in each slot. `right_roots`: symmetric in each slot.
All inputs are finite; a program needn't handle non-finite values.
Results may differ from a plain program's by a relative error of at most 0.0095.
Values may be sent and summed in bfloat16 or wider, within the bound.
No kernel may reach another device: no remote copies, remote signals or barrier semaphores. Data moves between devices by JAX's collectives and lax.ppermute only.
A program may use at most 256 MiB of HBM per device.

v0:
```python
import jax
import jax.numpy as jnp
from jax import lax
from jax.sharding import PartitionSpec as P

H = 12
HD = 64
ROT = 16
FF = 3072
norm_eps = 1e-05
floor_score = -1e30
rate_matrix = 0.03
rate_vector = 1.5
decay_vector = 0.9


def contract(first_op, second_op, first_dim, second_dim):
    return lax.dot_general(
        first_op,
        second_op,
        (((first_dim,), (second_dim,)), ((), ())),
        preferred_element_type=jnp.float32,
    )


def unblock(blocks, row_total, col_total):
    blk_size = blocks.shape[-1]
    return (
        blocks.reshape(row_total // blk_size, col_total // blk_size, blk_size, blk_size)
        .transpose(0, 2, 1, 3)
        .reshape(row_total, col_total)
    )


def to_blocks(matrix, blk_size):
    row_count, col_count = matrix.shape
    return (
        matrix.reshape(row_count // blk_size, blk_size, col_count // blk_size, blk_size)
        .transpose(0, 2, 1, 3)
        .reshape(-1, blk_size, blk_size)
    )


def rotate(values, cosine_tab, sine_tab, local_heads):
    tok_rows = values.shape[0]
    shaped = values.reshape(tok_rows, local_heads, HD)
    rot_half = ROT // 2
    lower_half = shaped[:, :, :rot_half]
    upper_half = shaped[:, :, rot_half:ROT]
    turned = jnp.concatenate(
        [
            lower_half * cosine_tab - upper_half * sine_tab,
            upper_half * cosine_tab + lower_half * sine_tab,
            shaped[:, :, ROT:],
        ],
        axis=2,
    )
    return turned.reshape(tok_rows, local_heads * HD)


def slice_rows(array, row_start, row_count):
    return lax.dynamic_slice_in_dim(array, row_start, row_count, 0)


def back_norm(gradient, gain_vec, normed_rows, inv_rows):
    scaled = gradient * gain_vec
    centered = scaled - jnp.mean(scaled, axis=1, keepdims=True)
    return inv_rows * (
        centered - normed_rows * jnp.mean(scaled * normed_rows, axis=1, keepdims=True)
    )


def on_device(
    tokens,
    cotangent,
    seq_ids,
    block_slot,
    masters,
    left_stats,
    right_stats,
    left_roots,
    right_roots,
    vectors,
    vector_momentum,
):
    tensor_ways = lax.axis_size("tensor")
    tensor_index = lax.axis_index("tensor")
    data_ways = lax.axis_size("dp")
    data_index = lax.axis_index("dp")
    tok_rows, model_width = tokens.shape
    blk_size = masters.shape[-1]
    slot_count = masters.shape[1]
    local_heads = H // tensor_ways
    width_qkv = 3 * model_width // tensor_ways
    width_heads = model_width // tensor_ways
    width_hidden = FF // tensor_ways
    blocks_qkv = model_width // blk_size * (width_qkv // blk_size)
    blocks_attn = width_heads // blk_size * (model_width // blk_size)
    blocks_in = model_width // blk_size * (width_hidden // blk_size)
    mark_two = blocks_qkv + blocks_attn
    mark_three = mark_two + blocks_in
    copies = masters[0].astype(jnp.bfloat16)
    gathered = lax.all_gather(copies, "dp", axis=0, tiled=True)
    picked = jnp.take(gathered, block_slot, axis=0)
    w_qkv = unblock(picked[:blocks_qkv], model_width, width_qkv)
    w_attn = unblock(picked[blocks_qkv:mark_two], width_heads, model_width)
    w_in = unblock(picked[mark_two:mark_three], model_width, width_hidden)
    w_out = unblock(picked[mark_three:], width_hidden, model_width)
    gain_one = vectors[0:model_width]
    bias_one = vectors[model_width : 2 * model_width]
    gain_two = vectors[2 * model_width : 3 * model_width]
    bias_two = vectors[3 * model_width : 4 * model_width]
    bias_qkv = lax.dynamic_slice_in_dim(
        vectors, 4 * model_width + tensor_index * width_qkv, width_qkv
    )
    bias_attn = vectors[7 * model_width : 8 * model_width]
    bias_in = lax.dynamic_slice_in_dim(
        vectors, 8 * model_width + tensor_index * width_hidden, width_hidden
    )
    bias_out = vectors[8 * model_width + FF : 9 * model_width + FF]
    places = jnp.arange(tok_rows, dtype=jnp.int32)
    seq_first = jnp.concatenate([places[:1] == 0, seq_ids[1:] != seq_ids[:-1]])
    seq_start = lax.cummax(jnp.where(seq_first, places, 0), axis=0)
    position = (places - seq_start).astype(jnp.float32)
    rot_half = ROT // 2
    inverse = 10000.0 ** (-(2.0 * jnp.arange(rot_half, dtype=jnp.float32)) / ROT)
    angles = position[:, None] * inverse[None, :]
    cosine_tab = jnp.cos(angles)[:, None, :]
    sine_tab = jnp.sin(angles)[:, None, :]
    tokens_f = tokens.astype(jnp.float32)
    row_mean = jnp.mean(tokens_f, axis=1, keepdims=True)
    centered = tokens_f - row_mean
    inv_std = lax.rsqrt(jnp.mean(centered * centered, axis=1, keepdims=True) + norm_eps)
    normed = centered * inv_std
    norm_one = (normed * gain_one + bias_one).astype(jnp.bfloat16)
    norm_two = (normed * gain_two + bias_two).astype(jnp.bfloat16)
    mixed_qkv = jnp.dot(norm_one, w_qkv, preferred_element_type=jnp.float32) + bias_qkv
    queries = (
        rotate(mixed_qkv[:, :width_heads], cosine_tab, sine_tab, local_heads)
        .astype(jnp.bfloat16)
        .reshape(tok_rows, local_heads, HD)
    )
    keys_rot = (
        rotate(mixed_qkv[:, width_heads : 2 * width_heads], cosine_tab, sine_tab, local_heads)
        .astype(jnp.bfloat16)
        .reshape(tok_rows, local_heads, HD)
    )
    values_all = (
        mixed_qkv[:, 2 * width_heads :].astype(jnp.bfloat16).reshape(tok_rows, local_heads, HD)
    )
    blk_rows = min(512, tok_rows)
    block_total = tok_rows // blk_rows
    score_scale = HD ** (-0.5)

    def block_scores(block_index):
        row_low = block_index * blk_rows
        row_high = row_low + blk_rows
        scores = (
            jnp.einsum(
                "qhe,khe->hqk",
                queries[row_low:row_high],
                keys_rot[:row_high],
                preferred_element_type=jnp.float32,
            )
            * score_scale
        )
        allowed = (seq_ids[row_low:row_high, None] == seq_ids[None, :row_high]) & (
            places[row_low:row_high, None] >= places[None, :row_high]
        )
        return jnp.where(allowed[None], scores, floor_score)

    outputs = []
    log_sums = []
    for block_index in range(block_total):
        key_span = (block_index + 1) * blk_rows
        scores = block_scores(block_index)
        row_max = jnp.max(scores, axis=2, keepdims=True)
        exp_scores = jnp.exp(scores - row_max)
        row_total = jnp.sum(exp_scores, axis=2, keepdims=True)
        weights_low = (exp_scores / row_total).astype(jnp.bfloat16)
        outputs.append(
            jnp.einsum(
                "hqk,khe->qhe",
                weights_low,
                values_all[:key_span],
                preferred_element_type=jnp.float32,
            )
        )
        log_sums.append(row_max + jnp.log(row_total))
    attended = jnp.concatenate(outputs, axis=0).reshape(tok_rows, width_heads).astype(jnp.bfloat16)
    pre_hidden = jnp.dot(norm_two, w_in, preferred_element_type=jnp.float32) + bias_in
    hidden = jax.nn.gelu(pre_hidden, approximate=False).astype(jnp.bfloat16)
    own_rows = tok_rows // tensor_ways
    row_base = tensor_index * own_rows
    row_start = jnp.int32(0)
    attn_part = slice_rows(attended, row_start, lax.axis_size("tensor") * own_rows)
    hidden_part = slice_rows(hidden, row_start, lax.axis_size("tensor") * own_rows)
    branch_total = lax.psum_scatter(
        (
            jnp.dot(attn_part, w_attn, preferred_element_type=jnp.float32)
            + jnp.dot(hidden_part, w_out, preferred_element_type=jnp.float32)
        ).astype(jnp.bfloat16),
        "tensor",
        scatter_dimension=0,
        tiled=True,
    ).astype(jnp.float32)
    tokens_own = slice_rows(tokens_f, row_base, own_rows)
    mixed = (tokens_own + branch_total + bias_attn + bias_out).astype(jnp.bfloat16)
    grad_out_w = contract(hidden, cotangent, 0, 0)
    grad_hidden = contract(cotangent, w_out, 1, 1)
    density = jnp.exp(-0.5 * pre_hidden * pre_hidden) * 0.3989422804014327
    slope = 0.5 * (1.0 + lax.erf(pre_hidden * 0.7071067811865476)) + pre_hidden * density
    grad_pre = (grad_hidden * slope).astype(jnp.bfloat16)
    grad_in_w = contract(norm_two, grad_pre, 0, 0)
    grad_norm_two = contract(grad_pre, w_in, 1, 1)
    grad_bias_in = jnp.sum(grad_pre.astype(jnp.float32), axis=0)
    grad_attn_w = contract(attended, cotangent, 0, 0)
    grad_attended = (
        contract(cotangent, w_attn, 1, 1).astype(jnp.bfloat16).reshape(tok_rows, local_heads, HD)
    )
    grad_queries = []
    grad_keys = jnp.zeros((tok_rows, local_heads, HD), jnp.float32)
    grad_values = jnp.zeros((tok_rows, local_heads, HD), jnp.float32)
    for block_index in range(block_total):
        row_low = block_index * blk_rows
        row_high = row_low + blk_rows
        scores = block_scores(block_index)
        prob_full = jnp.exp(scores - log_sums[block_index])
        prob_low = prob_full.astype(jnp.bfloat16)
        grad_probs = jnp.einsum(
            "qhe,khe->hqk",
            grad_attended[row_low:row_high],
            values_all[:row_high],
            preferred_element_type=jnp.float32,
        )
        row_delta = jnp.sum(prob_full * grad_probs, axis=2, keepdims=True)
        grad_scores = (prob_full * (grad_probs - row_delta)).astype(jnp.bfloat16)
        grad_queries.append(
            jnp.einsum(
                "hqk,khe->qhe", grad_scores, keys_rot[:row_high], preferred_element_type=jnp.float32
            )
            * score_scale
        )
        grad_keys = grad_keys.at[:row_high].add(
            jnp.einsum(
                "hqk,qhe->khe",
                grad_scores,
                queries[row_low:row_high],
                preferred_element_type=jnp.float32,
            )
            * score_scale
        )
        grad_values = grad_values.at[:row_high].add(
            jnp.einsum(
                "hqk,qhe->khe",
                prob_low,
                grad_attended[row_low:row_high],
                preferred_element_type=jnp.float32,
            )
        )
    grad_query_all = jnp.concatenate(grad_queries, axis=0).reshape(tok_rows, width_heads)
    grad_mixed = jnp.concatenate(
        [
            rotate(grad_query_all, cosine_tab, -sine_tab, local_heads),
            rotate(grad_keys.reshape(tok_rows, width_heads), cosine_tab, -sine_tab, local_heads),
            grad_values.reshape(tok_rows, width_heads),
        ],
        axis=1,
    ).astype(jnp.bfloat16)
    grad_qkv_w = contract(norm_one, grad_mixed, 0, 0)
    grad_norm_one = contract(grad_mixed, w_qkv, 1, 1)
    grad_bias_qkv = jnp.sum(grad_mixed.astype(jnp.float32), axis=0)
    row_start = jnp.int32(0)
    row_count = lax.axis_size("tensor") * own_rows
    normed_rows = slice_rows(normed, row_start, row_count)
    inv_rows = slice_rows(inv_std, row_start, row_count)
    input_part = lax.psum_scatter(
        (
            back_norm(
                slice_rows(grad_norm_one, row_start, row_count), gain_one, normed_rows, inv_rows
            )
            + back_norm(
                slice_rows(grad_norm_two, row_start, row_count), gain_two, normed_rows, inv_rows
            )
        ).astype(jnp.bfloat16),
        "tensor",
        scatter_dimension=0,
        tiled=True,
    ).astype(jnp.float32)
    cot_own = slice_rows(cotangent, row_base, own_rows).astype(jnp.float32)
    input_grad = cot_own + input_part
    bias_grad_out = jnp.sum(cot_own, axis=0)
    pieces = [
        jnp.sum(grad_norm_one * normed, axis=0),
        jnp.sum(grad_norm_one, axis=0),
        jnp.sum(grad_norm_two * normed, axis=0),
        jnp.sum(grad_norm_two, axis=0),
        lax.dynamic_update_slice_in_dim(
            jnp.zeros((3 * model_width,), jnp.float32), grad_bias_qkv, tensor_index * width_qkv, 0
        ),
        bias_grad_out,
        lax.dynamic_update_slice_in_dim(
            jnp.zeros((FF,), jnp.float32), grad_bias_in, tensor_index * width_hidden, 0
        ),
        bias_grad_out,
    ]
    vector_sum = lax.psum(jnp.concatenate(pieces), ("dp", "tensor"))
    grad_scale = 1.0 / jnp.sqrt(jnp.float32(data_ways * tok_rows))
    vector_grad = vector_sum * grad_scale
    new_momentum = decay_vector * vector_momentum + (1.0 - decay_vector) * vector_grad
    new_vectors = vectors - rate_vector * new_momentum
    local_blocks = jnp.concatenate(
        [
            to_blocks(grad_qkv_w, blk_size),
            to_blocks(grad_attn_w, blk_size),
            to_blocks(grad_in_w, blk_size),
            to_blocks(grad_out_w, blk_size),
        ],
        axis=0,
    )
    slot_total = data_ways * slot_count
    summed = lax.psum(local_blocks, "dp")
    owner_of = (
        jnp.full((slot_total,), -1, jnp.int32)
        .at[block_slot]
        .set(jnp.arange(block_slot.shape[0], dtype=jnp.int32))
    )
    mine_blocks = lax.dynamic_slice_in_dim(owner_of, data_index * slot_count, slot_count, 0)
    owned = jnp.where(
        (mine_blocks >= 0)[:, None, None],
        jnp.take(summed, jnp.maximum(mine_blocks, 0), axis=0),
        0.0,
    )
    grad_blocks = owned * grad_scale
    highest = lax.Precision.HIGHEST
    new_left = (
        0.5 * left_stats[0]
        + 0.5 * jnp.einsum("sij,skj->sik", grad_blocks, grad_blocks, precision=highest) / blk_size
    )
    new_right = (
        0.5 * right_stats[0]
        + 0.5 * jnp.einsum("sji,sjk->sik", grad_blocks, grad_blocks, precision=highest) / blk_size
    )
    update_step = jnp.einsum("sij,sjk->sik", left_roots[0], grad_blocks, precision=highest)
    update_step = jnp.einsum("sij,sjk->sik", update_step, right_roots[0], precision=highest)
    new_masters = masters[0] - rate_matrix * update_step
    return (
        mixed,
        input_grad,
        grad_blocks[None],
        new_masters[None],
        new_left[None],
        new_right[None],
        new_vectors,
        new_momentum,
    )


def solution(mesh):
    return jax.shard_map(
        on_device,
        mesh=mesh,
        in_specs=(
            P("dp", None),
            P("dp", None),
            P("dp"),
            P(),
            P("tensor", "dp", None, None),
            P("tensor", "dp", None, None),
            P("tensor", "dp", None, None),
            P("tensor", "dp", None, None),
            P("tensor", "dp", None, None),
            P(),
            P(),
        ),
        out_specs=(
            P(("dp", "tensor"), None),
            P(("dp", "tensor"), None),
            P("tensor", "dp", None, None),
            P("tensor", "dp", None, None),
            P("tensor", "dp", None, None),
            P("tensor", "dp", None, None),
            P(),
            P(),
        ),
        check_vma=False,
    )
```

profile of v0, /device:TPU:0, one launch (start us, length us, event | category | flops | bytes accessed | tf_op | source)
XLA Modules:
  0.0 953.4 jit_solution(12270465933401899179)
XLA Ops:
  28.0 88.9 %all-gather.2.cloned.1.call-done = bf16[224,128,128]{2,1,0:T(8,128)(2,1)} async-done(((bf16[14,128,128]{2,1,0:T(8,128)(2,1)}), bf16[224,128,128]{2,1,0:T(8,128)(2,1)}) %all-gather.2.cloned.1.call-update) | async-done | bytes 7340048 | tf_op jit(solution)/shard_map/all_gather | solution.py:103
  116.9 11.4 %gather_fusion = bf16[216,128,128]{2,1,0:T(8,128)(2,1)} fusion(bf16[224,128,128]{2,1,0:T(8,128)(2,1)} %all-gather.2.cloned.1.call-done, s32[1024]{0:T(1024)S(1)} %pad_clamp_fusion.1), kind=kCustom, calls=%fused_computation | custom fusion | bytes 14156640 | tf_op jit(solution)/shard_map/jit(_take)/gather | solution.py:104
  139.3 6.8 fusion.159
  185.5 6.2 multiply_reduce_fusion.2
  194.5 7.3 multiply_convert_fusion.2
  206.2 8.4 fusion.161
  214.7 9.0 fusion.2
  223.7 10.5 %fusion.53 = f32[2048,6,64]{0,2,1:T(8,128)} fusion(f32[2048,6,64]{0,2,1:T(8,128)} %copy-done.8, bf16[512,6,64]{0,2,1:T(8,128)(2,1)S(1)} %bitcast.244, f32[6,512,1536]{2,1,0:T(8,128)} %get-tuple-element.177, f32[6,512]{1,0:T(8,128)S(1)} %log_add_fusion.1), kind=kOutput, calls=%fused_computation.109 | convolution fusion | flops 614006784 | bytes 23998464 | tf_op jit(solution)/shard_map/hqk,qhe->khe/dot_general | solution.py:254
  234.2 12.1 %multiply_reduce_fusion.1 = (f32[6,512]{1,0:T(8,128)S(1)}, f32[6,512,1536]{2,1,0:T(8,128)}) fusion(f32[6,512,1536]{2,1,0:T(8,128)} %get-tuple-element.177, f32[6,512]{1,0:T(8,128)S(1)} %log_add_fusion.1, bf16[512,6,64]{0,2,1:T(8,128)(2,1)S(1)} %bitcast.245, bf16[1536,6,64]{0,2,1:T(8,128)(2,1)S(1)} %bitcast.241), kind=kOutput, calls=%fused_computation.14 | convolution fusion | flops 618132480 | bytes 39346176 | tf_op jit(solution)/shard_map/qhe,khe->hqk/dot_general | solution.py:230
  246.3 12.9 %multiply_convert_fusion.1 = bf16[6,512,1536]{2,1,0:T(8,128)(2,1)S(1)} fusion(f32[6,512,1536]{2,1,0:T(8,128)} %get-tuple-element.187, f32[6,512,1536]{2,1,0:T(8,128)} %get-tuple-element.177, f32[6,512]{1,0:T(8,128)S(1)} %get-tuple-element.186, f32[6,512]{1,0:T(8,128)S(1)} %log_add_fusion.1), kind=kLoop, calls=%fused_computation.13 | loop fusion | flops 18874368 | bytes 47210496 | tf_op jit(solution)/shard_map/convert_element_type | solution.py:237
  265.9 34.4 %fusion.6 = (bf16[2048,1536]{1,0:T(8,128)(2,1)S(1)}, f32[2048,1536]{1,0:T(8,128)}) fusion(f32[1536]{0:T(1024)S(1)} %copy-done.66, bf16[96,8,12,128]{3,2,1,0:T(8,128)(2,1)S(1)} %bitcast.253, bf16[2048,768]{1,0:T(8,128)(2,1)S(1)} %copy-done.2, f32[768]{0:T(1024)S(1)} %copy-done.70, f32[768]{0:T(1024)S(1)} %copy-done.65, f32[2048]{0:T(1024)S(1)} %add_rsqrt_fusion, ...), kind=kOutput, calls=%fused_computation.24 | convolution fusion | flops 5048893440 | bytes 24408064 | tf_op jit(solution)/shard_map/dot_general | solution.py:191
  300.4 13.2 %convert_reduce_fusion = (f32[1536]{0:T(1024)}, bf16[2048,1536]{1,0:T(8,128)(2,1)S(1)}) fusion(f32[2048,1536]{1,0:T(8,128)} %get-tuple-element.171, f32[1536]{0:T(1024)S(1)} %copy-done.66, bf16[2048,768]{1,0:T(8,128)(2,1)S(1)} %copy-done.19, bf16[192,8,6,128]{3,2,1,0:T(8,128)(2,1)S(1)} %bitcast.255), kind=kOutput, calls=%fused_computation.32 | convolution fusion | flops 4872731136 | bytes 24391680 | tf_op jit(solution)/shard_map/dot_general | solution.py:18
  313.6 7.0 fusion.60
  320.6 6.9 fusion.58
  327.5 10.7 %fusion.160 = (f32[6,512]{1,0:T(8,128)S(1)}, f32[6,512,2048]{2,1,0:T(8,128)}) fusion(bf16[2048,6,64]{0,2,1:T(8,128)(2,1)S(1)} %get-tuple-element.194, bf16[2048,6,64]{0,2,1:T(8,128)(2,1)S(1)} %copy-done.13, pred[512,2048]{1,0:T(8,128)(4,1)S(1)} %copy-done.17), kind=kOutput, calls=%fused_computation.283 | convolution fusion | flops 824177664 | bytes 28192768 | tf_op jit(solution)/shard_map/qhe,khe->hqk/dot_general | solution.py:159
  338.3 10.9 %fusion = f32[6,512]{1,0:T(8,128)S(1)} fusion(f32[6,512,2048]{2,1,0:T(8,128)} %get-tuple-element.175, f32[6,512]{1,0:T(8,128)S(1)} %get-tuple-element.174), kind=kLoop, calls=%fused_computation.9 | loop fusion | flops 12579840 | bytes 25190400 | tf_op jit(solution)/shard_map/reduce_sum | solution.py:179
  349.2 11.9 %fusion.39 = bf16[2048,6,64]{0,2,1:T(8,128)(2,1)} fusion(f32[2048,6,64]{0,2,1:T(8,128)S(1)} %copy-done.9, bf16[512,6,64]{0,2,1:T(8,128)(2,1)S(1)} %bitcast.242, f32[6,512,2048]{2,1,0:T(8,128)} %get-tuple-element.175, f32[6,512]{1,0:T(8,128)S(1)} %log_add_fusion), kind=kOutput, calls=%fused_computation.97 | convolution fusion | flops 819462144 | bytes 30289920 | tf_op jit(solution)/shard_map/hqk,qhe->khe/dot_general | solution.py:254
  361.1 19.5 %multiply_reduce_fusion = (f32[6,512]{1,0:T(8,128)S(1)}, f32[6,512,2048]{2,1,0:T(8,128)}) fusion(f32[6,512,2048]{2,1,0:T(8,128)} %get-tuple-element.175, f32[6,512]{1,0:T(8,128)S(1)} %log_add_fusion, bf16[512,6,64]{0,2,1:T(8,128)(2,1)S(1)} %bitcast.243, bf16[2048,6,64]{0,2,1:T(8,128)(2,1)S(1)} %bitcast.227), kind=kOutput, calls=%fused_computation.4 | convolution fusion | flops 824177664 | bytes 52322304 | tf_op jit(solution)/shard_map/qhe,khe->hqk/dot_general | solution.py:230
  380.6 16.9 %multiply_convert_fusion = bf16[6,512,2048]{2,1,0:T(8,128)(2,1)S(1)} fusion(f32[6,512,2048]{2,1,0:T(8,128)} %get-tuple-element.189, f32[6,512,2048]{2,1,0:T(8,128)} %get-tuple-element.175, f32[6,512]{1,0:T(8,128)S(1)} %get-tuple-element.188, f32[6,512]{1,0:T(8,128)S(1)} %log_add_fusion), kind=kLoop, calls=%fused_computation.3 | loop fusion | flops 25165824 | bytes 62939136 | tf_op jit(solution)/shard_map/convert_element_type | solution.py:237
  412.1 11.4 %multiply_reduce_fusion.4 = (f32[768]{0:T(1024)S(1)}, f32[2048]{0:T(1024)S(1)}, f32[2048]{0:T(1024)S(1)}, f32[768]{0:T(1024)S(1)}, f32[768]{0:T(1024)S(1)}, /*in...) fusion(bf16[2048,768]{1,0:T(8,128)(2,1)S(1)} %copy-done.3, ...), kind=kOutput, calls=%fused_computation.67 | convolution fusion | flops 3664761856 | bytes 22284288 | tf_op jit(solution)/shard_map/dot_general | solution.py:18
  423.6 6.5 multiply_convert_fusion.3
  430.3 9.9 %fusion.100 = bf16[6,64,512]{2,1,0:T(8,128)(2,1)S(1)} fusion(bf16[1536,6,64]{0,2,1:T(8,128)(2,1)} %bitcast.240, f32[6,512,1536]{2,1,0:T(8,128)} %get-tuple-element.177, f32[6,512]{1,0:T(8,128)S(1)} %copy-done.59, f32[6,512]{1,0:T(8,128)S(1)} %copy-done.57), kind=kOutput, calls=%fused_computation.169 | convolution fusion | flops 618332160 | bytes 20471808 | tf_op jit(solution)/shard_map/hqk,khe->qhe/dot_general | solution.py:182
  440.2 10.7 %fusion.101 = bf16[6,64,512]{2,1,0:T(8,128)(2,1)S(1)} fusion(bf16[2048,6,64]{0,2,1:T(8,128)(2,1)S(1)} %bitcast.228, f32[6,512,2048]{2,1,0:T(8,128)} %get-tuple-element.175, f32[6,512]{1,0:T(8,128)S(1)} %fusion, f32[6,512]{1,0:T(8,128)S(1)} %get-tuple-element.174), kind=kOutput, calls=%fused_computation.170 | convolution fusion | flops 824377344 | bytes 27156480 | tf_op jit(solution)/shard_map/hqk,khe->qhe/dot_general | solution.py:182
  460.3 11.8 %fusion.153 = f32[768,1536]{1,0:T(8,128)} fusion(bf16[2048,1536]{1,0:T(8,128)(2,1)} %copy-done.74, bf16[2048,768]{1,0:T(8,128)(2,1)} %param.31, f32[768]{0:T(1024)S(1)} %copy-done.71, f32[768]{0:T(1024)S(1)} %copy-done.65, f32[2048]{0:T(1024)S(1)} %add_rsqrt_fusion, f32[2048]{0:T(1024)S(1)} %broadcast_multiply_fusion.4), kind=kOutput, calls=%fused_computation.276 | convolution fusion | flops 4841275392 | bytes 14178304 | tf_op jit(solution)/shard_map/dot_general | solution.py:18
  472.1 6.7 reshape.811
  478.8 6.7 copy.53
  485.4 8.7 fusion.165
  494.1 6.8 reshape.813
  506.9 6.1 fusion.152
  528.8 7.8 pad_maximum_fusion
  551.0 42.9 %psum.15 = f32[9984]{0:T(1024)S(1)} all-reduce(f32[9984]{0:T(1024)S(1)} %constant_dynamic-update-slice_fusion), channel_id=1, replica_groups=mesh['dp'=16,'tensor'=2] {'dp','tensor'}, use_global_device_ids=true, to_apply=%region_31.32 | all-reduce | flops 9984 | bytes 79872 | tf_op jit(solution)/shard_map/psum | solution.py:307
  598.7 329.6 %all-reduce.4.cloned.1.call-done = f32[216,128,128]{2,1,0:T(8,128)} async-done(((f32[216,128,128]{2,1,0:T(8,128)}), f32[216,128,128]{2,1,0:T(8,128)}) %all-reduce.4.cloned.1.call-update) | async-done | bytes 14155792 | tf_op jit(solution)/shard_map/psum | solution.py:322
  (299 shorter events, 167.2 us)
Async XLA Ops:
  7.2 936.1 %copy-start = (f32[1,14,128,128]{3,2,1,0:T(8,128)S(1)}, f32[1,14,128,128]{3,2,1,0:T(8,128)}, u32[]{:S(2)}) copy-start(f32[1,14,128,128]{3,2,1,0:T(8,128)} %param.38) | copy-start | bytes 2752516
  7.2 14.8 %slice-start.5 = ((s32[2048]{0:T(1024)}), s32[1024]{0:T(1024)S(1)}, s32[]{:S(2)}) async-start(s32[2048]{0:T(1024)} %param.33), calls=%async_computation.11 | async-start | bytes 8192 | tf_op jit(solution)/shard_map/slice | solution.py:167
  7.2 17.1 %copy-start.53 = (s32[2048]{0:T(1024)S(1)}, s32[2048]{0:T(1024)}, u32[]{:S(2)}) copy-start(s32[2048]{0:T(1024)} %param.33) | copy-start | bytes 24580
  7.2 13.9 %copy-start.54 = (f32[9984]{0:T(1024)S(1)}, f32[9984]{0:T(1024)}, u32[]{:S(2)}) copy-start(f32[9984]{0:T(1024)} %param.40) | copy-start | bytes 119812
  7.2 109.7 %all-gather.2.cloned.1.call-start = ((), (), s32[]{:S(2)}) async-start(), calls=%async_computation.2 | async-start | bytes 7798784 | tf_op jit(solution)/shard_map/all_gather | solution.py:103
  9.4 537.5 %reduce-scatter.5.cloned.1.call-start = ((), (), s32[]{:S(2)}) async-start(), calls=%async_computation.4 | async-start | bytes 4718592 | tf_op jit(solution)/shard_map/reduce_scatter | solution.py:277
  21.7 117.6 %copy-start.63 = (f32[768]{0:T(1024)}, f32[768]{0:T(1024)S(1)}, u32[]{:S(2)}) copy-start(f32[768]{0:T(1024)S(1)} %get-tuple-element.160) | copy-start | bytes 9220
  21.7 117.6 %copy-start.68 = (f32[768]{0:T(1024)}, f32[768]{0:T(1024)S(1)}, u32[]{:S(2)}) copy-start(f32[768]{0:T(1024)S(1)} %get-tuple-element.159) | copy-start | bytes 9220
  24.2 123.0 %copy-start.43 = (f32[2048,8]{0,1:T(8,128)}, f32[2048,8]{0,1:T(8,128)S(1)}, u32[]{:S(2)}) copy-start(f32[2048,8]{0,1:T(8,128)S(1)} %get-tuple-element.164) | copy-start | bytes 196612
  154.1 173.4 %copy-start.1 = (bf16[2048,6,64]{0,2,1:T(8,128)(2,1)}, bf16[2048,6,64]{0,2,1:T(8,128)(2,1)S(1)}, u32[]{:S(2)}) copy-start(bf16[2048,6,64]{0,2,1:T(8,128)(2,1)S(1)} %get-tuple-element.194) | copy-start | bytes 4718596
  264.9 35.5 %copy-start.7 = (f32[2048,6,64]{0,2,1:T(8,128)}, f32[2048,6,64]{0,2,1:T(8,128)S(1)}, u32[]{:S(2)}) copy-start(f32[2048,6,64]{0,2,1:T(8,128)S(1)} %fusion.46) | copy-start | bytes 9437188
  265.9 34.5 %copy-start.19 = (bf16[2048,768]{1,0:T(8,128)(2,1)S(1)}, bf16[2048,768]{1,0:T(8,128)(2,1)}, u32[]{:S(2)}) copy-start(bf16[2048,768]{1,0:T(8,128)(2,1)} %param.32) | copy-start | bytes 9437188
  265.9 34.5 %copy-start.38 = (bf16[12,6,128,128]{3,1,2,0:T(8,128)(2,1)S(1)}, bf16[12,6,128,128]{3,1,2,0:T(8,128)(2,1)}, u32[]{:S(2)}) copy-start(bf16[12,6,128,128]{3,1,2,0:T(8,128)(2,1)} %copy.45) | copy-start | bytes 7077892
  300.4 20.2 %copy-start.73 = (bf16[2048,1536]{1,0:T(8,128)(2,1)}, bf16[2048,1536]{1,0:T(8,128)(2,1)S(1)}, u32[]{:S(2)}) copy-start(bf16[2048,1536]{1,0:T(8,128)(2,1)S(1)} %get-tuple-element.170) | copy-start | bytes 18874372
  338.3 10.9 %copy-start.31 = (bf16[512,384]{0,1:T(8,128)(2,1)S(1)}, bf16[512,384]{0,1:T(8,128)(2,1)}, u32[]{:S(2)}) copy-start(bf16[512,384]{0,1:T(8,128)(2,1)} %get-tuple-element.150) | copy-start | bytes 1179652
  349.2 12.0 %copy-start.21 = (bf16[2048,384]{0,1:T(8,128)(2,1)S(1)}, bf16[2048,384]{0,1:T(8,128)(2,1)}, u32[]{:S(2)}) copy-start(bf16[2048,384]{0,1:T(8,128)(2,1)} %slice.514) | copy-start | bytes 4718596
  408.5 15.1 %slice-start.3 = ((s8[6291456]{0:T(1024)(128)(4,1)}), s8[4194304]{0:T(1024)(128)(4,1)S(1)}, s32[]{:S(2)}) async-start(s8[6291456]{0:T(1024)(128)(4,1)} %bitcast.232), calls=%async_computation.9 | async-start | bytes 8388608
  408.6 14.9 %copy-start.25 = (bf16[2048,6,64]{0,2,1:T(8,128)(2,1)}, bf16[2048,6,64]{0,2,1:T(8,128)(2,1)S(1)}, u32[]{:S(2)}) copy-start(bf16[2048,6,64]{0,2,1:T(8,128)(2,1)S(1)} %pad_maximum_fusion.4) | copy-start | bytes 4718596
  408.8 14.7 %copy-start.27 = (bf16[2048,6,64]{0,2,1:T(8,128)(2,1)}, bf16[2048,6,64]{0,2,1:T(8,128)(2,1)S(1)}, u32[]{:S(2)}) copy-start(bf16[2048,6,64]{0,2,1:T(8,128)(2,1)S(1)} %pad_maximum_fusion.5) | copy-start | bytes 4718596
  412.1 11.4 %slice-start.4 = ((s8[6291456]{0:T(1024)(128)(4,1)}), s8[2097152]{0:T(1024)(128)(4,1)S(1)}, s32[]{:S(2)}) async-start(s8[6291456]{0:T(1024)(128)(4,1)} %bitcast.232), calls=%async_computation.10 | async-start | bytes 4194304
  430.2 163.7 %reduce-scatter.3.cloned.1.call-start = ((), (), s32[]{:S(2)}) async-start(), calls=%async_computation.3 | async-start | bytes 4718592 | tf_op jit(solution)/shard_map/reduce_scatter | solution.py:198
  430.2 21.4 %slice-start.6 = ((s8[6291456]{0:T(1024)(128)(4,1)}), s8[4194304]{0:T(1024)(128)(4,1)S(1)}, s32[]{:S(2)}) async-start(s8[6291456]{0:T(1024)(128)(4,1)} %bitcast.274), calls=%async_computation.12 | async-start | bytes 8388608
  440.2 11.5 %copy-start.47 = (bf16[3,6,128,128]{3,1,2,0:T(8,128)(2,1)S(1)}, bf16[3,6,128,128]{3,1,2,0:T(8,128)(2,1)}, u32[]{:S(2)}) copy-start(bf16[3,6,128,128]{3,1,2,0:T(8,128)(2,1)} %copy-done.46) | copy-start | bytes 1769476
  440.2 11.5 %copy-start.48 = (bf16[6,64,512]{2,1,0:T(8,128)(2,1)S(1)}, bf16[6,64,512]{2,1,0:T(8,128)(2,1)}, u32[]{:S(2)}) copy-start(bf16[6,64,512]{2,1,0:T(8,128)(2,1)} %fusion.98) | copy-start | bytes 1179652
  440.2 11.5 %copy-start.49 = (bf16[6,64,512]{2,1,0:T(8,128)(2,1)S(1)}, bf16[6,64,512]{2,1,0:T(8,128)(2,1)}, u32[]{:S(2)}) copy-start(bf16[6,64,512]{2,1,0:T(8,128)(2,1)} %fusion.99) | copy-start | bytes 1179652
  440.2 11.5 %slice-start.7 = ((s8[6291456]{0:T(1024)(128)(4,1)}), s8[2097152]{0:T(1024)(128)(4,1)S(1)}, s32[]{:S(2)}) async-start(s8[6291456]{0:T(1024)(128)(4,1)} %bitcast.274), calls=%async_computation.13 | async-start | bytes 4194304
  455.3 472.9 %all-reduce.4.cloned.1.call-start = ((), (), s32[]{:S(2)}) async-start(), calls=%async_computation.5 | async-start | bytes 28311552 | tf_op jit(solution)/shard_map/psum | solution.py:322
  542.3 51.6 %copy-start.61 = (f32[768]{0:T(1024)S(1)}, f32[768]{0:T(1024)}, u32[]{:S(2)}) copy-start(f32[768]{0:T(1024)} %get-tuple-element.156) | copy-start | bytes 9220
  542.3 51.7 %copy-start.62 = (f32[768]{0:T(1024)S(1)}, f32[768]{0:T(1024)}, u32[]{:S(2)}) copy-start(f32[768]{0:T(1024)} %get-tuple-element.161) | copy-start | bytes 9220
  546.9 51.1 %copy-start.55 = (f32[9984]{0:T(1024)S(1)}, f32[9984]{0:T(1024)}, u32[]{:S(2)}) copy-start(f32[9984]{0:T(1024)} %param.40) | copy-start | bytes 119812
  546.9 51.1 %copy-start.60 = (f32[9984]{0:T(1024)S(1)}, f32[9984]{0:T(1024)}, u32[]{:S(2)}) copy-start(f32[9984]{0:T(1024)} %param.41) | copy-start | bytes 119812
  598.0 346.4 %copy-start.30 = (f32[1,14,128,128]{3,2,1,0:T(8,128)S(1)}, f32[1,14,128,128]{3,2,1,0:T(8,128)}, u32[]{:S(2)}) copy-start(f32[1,14,128,128]{3,2,1,0:T(8,128)} %param.35) | copy-start | bytes 2752516
  (55 other events, 281.3 us)
Sparse Core Ops, SparseCore 0:
  11.3 105.5 all-gather.1
  430.3 9.4 reduce-scatter.4
  455.4 9.4 reduce-scatter.2
  536.8 391.3 all-reduce.3
where the time goes:
time: 962 us; the launch traced here: 953 us
  waiting for transfers between devices  419 us (44%)
  matrix products  267 us (28%)
  other arithmetic  119 us (12%)
  local copies, waits for them, and re-layouts  90.4 us (9%)
  blocking collectives  42.9 us (4%)
  between operations  15.6 us (2%)
    psum x1, waiting for transfers between devices, on_device(): summed = lax.psum(local_blocks, 'dp')  330 us
    all_gather x1, waiting for transfers between devices, on_device(): gathered = lax.all_gather(copies, 'dp', axis=0, tiled=True)  88.9 us
    dot_general x8, matrix products, contract(): lax.dot_general(first_op, second_op, (((first_dim,), (second_dim,)), ((),...  63.7 us
    psum x1, blocking collectives, on_device(): vector_sum = lax.psum(jnp.concatenate(pieces), ('dp', 'tensor'))  42.9 us
    convert_element_type x4, other arithmetic, on_device(): grad_scores = (prob_full * (grad_probs - row_delta)).astype(jnp.bfloat16)  39.5 us
    dot_general x4, matrix products, on_device(): jnp.einsum('qhe,khe->hqk', grad_attended[row_low:row_high], values_all[:r...  39.1 us
    dot_general x1, matrix products, on_device(): jnp.dot(norm_two, w_in, preferred_element_type=jnp.float32) + bias_in  34.4 us
    dot_general x4, matrix products, on_device(): jnp.einsum('hqk,qhe->khe', prob_low, grad_attended[row_low:row_high], pre...  27.2 us
  transfers between devices with their start and end apart: 4, of which 2 were waited for; matrix products, arithmetic and copies ran while one was open for 15% of the time, Pallas kernels for 0%

commit v1 on v0

--- a/solution.py
+++ b/solution.py
@@ -319,7 +319,9 @@
         axis=0,
     )
     slot_total = data_ways * slot_count
-    summed = lax.psum(local_blocks, "dp")
+    summed = local_blocks
+    for hop in (1, 2, 4, 8):
+        summed = summed + lax.ppermute(summed, "dp", [(dev, dev ^ hop) for dev in range(16)])
     owner_of = (
         jnp.full((slot_total,), -1, jnp.int32)
         .at[block_slot]

time: 962 us -> 2120 us (2.20)
  blocking collectives: 42.9 us -> 596 us
  waiting for transfers between devices: 419 us -> 968 us
  other arithmetic: 119 us -> 156 us
    ppermute x0 -> x4, waiting for transfers between devices: none -> 881 us  [on_device(): lax.ppermute(summed, 'dp', [(dev, dev ^ hop) for dev in range(16)])]
    psum x1, blocking collectives: 42.9 us -> 596 us  [on_device(): vector_sum = lax.psum(jnp.concatenate(pieces), ('dp', 'tensor'))]
    psum x1 -> x0, waiting for transfers between devices: 330 us -> none  [on_device(): summed = lax.psum(local_blocks, 'dp')]
    add x0 -> x4, other arithmetic: none -> 45.4 us  [on_device(): summed + lax.ppermute(summed, 'dp', [(dev, dev ^ hop) for dev in range(16)])]
  transfers between devices with their start and end apart: 4 -> 7, of which waited for: 2 -> 4; matrix products, arithmetic and copies ran while one was open for 15% -> 4% of each run, Pallas kernels for 0% -> 0%
where the time goes in v1:
time: 2120 us; the launch traced here: 2110 us
  waiting for transfers between devices  968 us (46%)
  blocking collectives  596 us (28%)
  matrix products  268 us (13%)
  other arithmetic  156 us (7%)
  local copies, waits for them, and re-layouts  95.7 us (5%)
    ppermute x4, waiting for transfers between devices, on_device(): lax.ppermute(summed, 'dp', [(dev, dev ^ hop) for dev in range(16)])  881 us
    psum x1, blocking collectives, on_device(): vector_sum = lax.psum(jnp.concatenate(pieces), ('dp', 'tensor'))  596 us
    all_gather x1, waiting for transfers between devices, on_device(): gathered = lax.all_gather(copies, 'dp', axis=0, tiled=True)  86.3 us
    dot_general x8, matrix products, contract(): lax.dot_general(first_op, second_op, (((first_dim,), (second_dim,)), ((),...  61.3 us
    add x4, other arithmetic, on_device(): summed + lax.ppermute(summed, 'dp', [(dev, dev ^ hop) for dev in range(16)])  45.4 us
  transfers between devices with their start and end apart: 7, of which 4 were waited for; matrix products, arithmetic and copies ran while one was open for 4% of the time, Pallas kernels for 0%

profile of v1, /device:TPU:0, one launch (start us, length us, event | category | flops | bytes accessed | tf_op | source)
XLA Modules:
  0.0 2107.5 jit_solution(10009426801010195366)
XLA Ops:
  30.6 86.3 %all-gather.2.cloned.1.call-done = bf16[224,128,128]{2,1,0:T(8,128)(2,1)} async-done(((bf16[14,128,128]{2,1,0:T(8,128)(2,1)}), bf16[224,128,128]{2,1,0:T(8,128)(2,1)}) %all-gather.2.cloned.1.call-update) | async-done | bytes 7340048 | tf_op jit(solution)/shard_map/all_gather | solution.py:103
  116.9 11.4 gather_fusion
  139.3 6.8 fusion.160
  194.4 7.3 multiply_convert_fusion.2
  206.1 8.5 fusion.162
  214.6 9.0 fusion.2
  223.6 9.4 fusion.100
  233.0 12.5 multiply_reduce_fusion.1
  245.5 8.1 fusion.53
  255.2 12.9 multiply_convert_fusion.1
  275.0 34.9 %fusion.6 = (bf16[2048,1536]{1,0:T(8,128)(2,1)}, f32[2048,1536]{1,0:T(8,128)}) fusion(f32[1536]{0:T(1024)S(1)} %copy-done.68, bf16[96,8,12,128]{3,2,1,0:T(8,128)(2,1)S(1)} %bitcast.264, bf16[2048,768]{1,0:T(8,128)(2,1)S(1)} %copy-done.3, f32[768]{0:T(1024)S(1)} %copy-done.71, f32[768]{0:T(1024)S(1)} %copy-done.63, f32[2048]{0:T(1024)S(1)} %copy-done.60, ...), kind=kOutput, calls=%fused_computation.24 | convolution fusion | flops 5048893440 | bytes 24408064 | tf_op jit(solution)/shard_map/dot_general | solution.py:191
  310.0 11.6 convert_reduce_fusion
  324.2 7.3 fusion.153
  331.5 6.7 reshape.811
  344.7 8.7 fusion.166
  365.9 11.7 fusion.161
  377.6 10.5 fusion
  388.2 11.8 fusion.101
  399.9 19.5 multiply_reduce_fusion
  419.4 12.6 fusion.39
  432.1 16.7 multiply_convert_fusion
  490.7 303.0 %collective-permute-done = f32[216,128,128]{2,1,0:T(8,128)} collective-permute-done((f32[216,128,128]{2,1,0:T(8,128)S(1)}, f32[216,128,128]{2,1,0:T(8,128)}, u32[]{:S(2)}, u32[]{:S(2)}) %collective-permute-start) | collective-permute-done | bytes 14155808 | tf_op jit(solution)/shard_map/ppermute | solution.py:324
  793.8 8.5 fusion.154
  808.1 297.9 %collective-permute-done.1 = f32[216,128,128]{2,1,0:T(8,128)} collective-permute-done((f32[216,128,128]{2,1,0:T(8,128)S(1)}, f32[216,128,128]{2,1,0:T(8,128)}, u32[]{:S(2)}, u32[]{:S(2)}) %collective-permute-start.1) | collective-permute-done | bytes 14155808 | tf_op jit(solution)/shard_map/ppermute | solution.py:324
  1106.0 10.3 add.292
  1116.4 9.9 fusion.60
  1126.4 12.3 multiply_reduce_fusion.4
  1138.7 280.4 %collective-permute-done.2 = f32[216,128,128]{2,1,0:T(8,128)} collective-permute-done((f32[216,128,128]{2,1,0:T(8,128)S(1)}, f32[216,128,128]{2,1,0:T(8,128)}, u32[]{:S(2)}, u32[]{:S(2)}) %collective-permute-start.2) | collective-permute-done | bytes 14155808 | tf_op jit(solution)/shard_map/ppermute | solution.py:324
  1419.1 12.1 add.293
  1440.4 8.5 fusion.58
  1466.7 596.3 %psum.7 = f32[9984]{0:T(1024)S(1)} all-reduce(f32[9984]{0:T(1024)S(1)} %constant_dynamic-update-slice_fusion), channel_id=1, replica_groups=mesh['dp'=16,'tensor'=2] {'dp','tensor'}, use_global_device_ids=true, to_apply=%region_30.31 | all-reduce | flops 9984 | bytes 79872 | tf_op jit(solution)/shard_map/psum | solution.py:307
  2067.6 14.6 add.294
  (313 shorter events, 213.9 us)
Async XLA Ops:
  7.2 2090.2 %copy-start = (f32[1,14,128,128]{3,2,1,0:T(8,128)S(1)}, f32[1,14,128,128]{3,2,1,0:T(8,128)}, u32[]{:S(2)}) copy-start(f32[1,14,128,128]{3,2,1,0:T(8,128)} %param.38) | copy-start | bytes 2752516
  7.2 109.7 %all-gather.2.cloned.1.call-start = ((), (), s32[]{:S(2)}) async-start(), calls=%async_computation.2 | async-start | bytes 7798784 | tf_op jit(solution)/shard_map/all_gather | solution.py:103
  9.4 1453.0 %reduce-scatter.5.cloned.1.call-start = ((), (), s32[]{:S(2)}) async-start(), calls=%async_computation.4 | async-start | bytes 4718592 | tf_op jit(solution)/shard_map/reduce_scatter | solution.py:277
  12.9 11.6 slice-start.9
  20.4 118.8 %copy-start.56 = (f32[2048]{0:T(1024)}, f32[2048]{0:T(1024)S(1)}, u32[]{:S(2)}) copy-start(f32[2048]{0:T(1024)S(1)} %broadcast_multiply_fusion.4) | copy-start | bytes 24580
  23.5 115.7 %copy-start.59 = (f32[2048]{0:T(1024)}, f32[2048]{0:T(1024)S(1)}, u32[]{:S(2)}) copy-start(f32[2048]{0:T(1024)S(1)} %add_rsqrt_fusion) | copy-start | bytes 24580
  24.2 115.0 %copy-start.65 = (f32[768]{0:T(1024)}, f32[768]{0:T(1024)S(1)}, u32[]{:S(2)}) copy-start(f32[768]{0:T(1024)S(1)} %get-tuple-element.160) | copy-start | bytes 9220
  24.2 115.0 %copy-start.69 = (f32[768]{0:T(1024)}, f32[768]{0:T(1024)S(1)}, u32[]{:S(2)}) copy-start(f32[768]{0:T(1024)S(1)} %get-tuple-element.159) | copy-start | bytes 9220
  26.8 120.4 %copy-start.41 = (f32[2048,8]{0,1:T(8,128)}, f32[2048,8]{0,1:T(8,128)S(1)}, u32[]{:S(2)}) copy-start(f32[2048,8]{0,1:T(8,128)S(1)} %get-tuple-element.164) | copy-start | bytes 196612
  154.1 211.8 %copy-start.1 = (bf16[2048,6,64]{0,2,1:T(8,128)(2,1)}, bf16[2048,6,64]{0,2,1:T(8,128)(2,1)S(1)}, u32[]{:S(2)}) copy-start(bf16[2048,6,64]{0,2,1:T(8,128)(2,1)S(1)} %get-tuple-element.194) | copy-start | bytes 4718596
  233.0 12.5 copy-start.10
  274.9 35.0 %copy-start.8 = (f32[2048,6,64]{0,2,1:T(8,128)}, f32[2048,6,64]{0,2,1:T(8,128)S(1)}, u32[]{:S(2)}) copy-start(f32[2048,6,64]{0,2,1:T(8,128)S(1)} %fusion.46) | copy-start | bytes 9437188
  275.0 35.0 %copy-start.20 = (bf16[2048,768]{1,0:T(8,128)(2,1)S(1)}, bf16[2048,768]{1,0:T(8,128)(2,1)}, u32[]{:S(2)}) copy-start(bf16[2048,768]{1,0:T(8,128)(2,1)} %param.32) | copy-start | bytes 9437188
  275.0 35.0 %copy-start.35 = (bf16[12,6,128,128]{3,1,2,0:T(8,128)(2,1)S(1)}, bf16[12,6,128,128]{3,1,2,0:T(8,128)(2,1)}, u32[]{:S(2)}) copy-start(bf16[12,6,128,128]{3,1,2,0:T(8,128)(2,1)} %copy.45) | copy-start | bytes 7077892
  388.2 11.8 copy-start.29
  480.5 313.3 %slice-start.2 = ((s8[4718592]{0:T(1024)(128)(4,1)}), s8[4194304]{0:T(1024)(128)(4,1)S(1)}, s32[]{:S(2)}) async-start(s8[4718592]{0:T(1024)(128)(4,1)} %bitcast.216), calls=%async_computation.7 | async-start | bytes 8388608
  484.6 309.1 %slice-start.3 = ((s8[4718592]{0:T(1024)(128)(4,1)}), s8[524288]{0:T(1024)(128)(4,1)S(1)}, s32[]{:S(2)}) async-start(s8[4718592]{0:T(1024)(128)(4,1)} %bitcast.216), calls=%async_computation.8 | async-start | bytes 1048576
  489.2 304.5 %collective-permute-start = (f32[216,128,128]{2,1,0:T(8,128)S(1)}, f32[216,128,128]{2,1,0:T(8,128)}, u32[]{:S(2)}, u32[]{:S(2)}) collective-permute-start(f32[216,128,128]{2,1,0:T(8,128)S(1)} %pad_maximum_fusion), channel_id=1, source_target_pairs={{0,2},{2,0},{4,6},{6,4},{8,10},{10,8},{12,14},{14,12},{16,18},{18,... | collective-permute-start | bytes 42467336 | tf_op jit(solution)/shard_map/ppermute | solution.py:324
  802.3 314.1 %copy-start.37 = (bf16[6,12,128,128]{3,1,2,0:T(8,128)(2,1)S(1)}, bf16[6,12,128,128]{3,1,2,0:T(8,128)(2,1)}, u32[]{:S(2)}) copy-start(bf16[6,12,128,128]{3,1,2,0:T(8,128)(2,1)} %copy.44) | copy-start | bytes 7077892
  802.3 303.7 %collective-permute-start.1 = (f32[216,128,128]{2,1,0:T(8,128)S(1)}, f32[216,128,128]{2,1,0:T(8,128)}, u32[]{:S(2)}, u32[]{:S(2)}) collective-permute-start(f32[216,128,128]{2,1,0:T(8,128)S(1)} %fusion.154), channel_id=1, source_target_pairs={{0,4},{2,6},{4,0},{6,2},{8,12},{10,14},{12,8},{14,10},{16,20},{18,... | collective-permute-start | bytes 42467336 | tf_op jit(solution)/shard_map/ppermute | solution.py:324
  1116.3 302.8 %collective-permute-start.2 = (f32[216,128,128]{2,1,0:T(8,128)S(1)}, f32[216,128,128]{2,1,0:T(8,128)}, u32[]{:S(2)}, u32[]{:S(2)}) collective-permute-start(f32[216,128,128]{2,1,0:T(8,128)S(1)} %add.292), channel_id=1, source_target_pairs={{0,8},{2,10},{4,12},{6,14},{8,0},{10,2},{12,4},{14,6},{16,24},{18,... | collective-permute-start | bytes 42467336 | tf_op jit(solution)/shard_map/ppermute | solution.py:324
  1138.7 297.4 %slice-start.5 = ((s8[6291456]{0:T(1024)(128)(4,1)}), s8[4194304]{0:T(1024)(128)(4,1)S(1)}, s32[]{:S(2)}) async-start(s8[6291456]{0:T(1024)(128)(4,1)} %bitcast.237), calls=%async_computation.10 | async-start | bytes 8388608
  1138.7 297.4 %slice-start.7 = ((s8[6291456]{0:T(1024)(128)(4,1)}), s8[4194304]{0:T(1024)(128)(4,1)S(1)}, s32[]{:S(2)}) async-start(s8[6291456]{0:T(1024)(128)(4,1)} %bitcast.239), calls=%async_computation.12 | async-start | bytes 8388608
  1138.7 297.3 %slice-start.6 = ((s8[6291456]{0:T(1024)(128)(4,1)}), s8[2097152]{0:T(1024)(128)(4,1)S(1)}, s32[]{:S(2)}) async-start(s8[6291456]{0:T(1024)(128)(4,1)} %bitcast.237), calls=%async_computation.11 | async-start | bytes 4194304
  1138.7 297.3 %slice-start.8 = ((s8[6291456]{0:T(1024)(128)(4,1)}), s8[2097152]{0:T(1024)(128)(4,1)S(1)}, s32[]{:S(2)}) async-start(s8[6291456]{0:T(1024)(128)(4,1)} %bitcast.239), calls=%async_computation.13 | async-start | bytes 4194304
  1431.2 636.5 %collective-permute-start.3 = (f32[216,128,128]{2,1,0:T(8,128)}, f32[216,128,128]{2,1,0:T(8,128)}, u32[]{:S(2)}, u32[]{:S(2)}) collective-permute-start(f32[216,128,128]{2,1,0:T(8,128)} %add.293), channel_id=1, source_target_pairs={{0,16},{2,18},{4,20},{6,22},{8,24},{10,26},{12,28},{14,30},{16,0},... | collective-permute-start | bytes 42467336 | tf_op jit(solution)/shard_map/ppermute | solution.py:324
  1440.3 622.6 %reduce-scatter.3.cloned.1.call-start = ((), (), s32[]{:S(2)}) async-start(), calls=%async_computation.3 | async-start | bytes 4718592 | tf_op jit(solution)/shard_map/reduce_scatter | solution.py:198
  1457.7 605.3 %copy-start.61 = (f32[768]{0:T(1024)S(1)}, f32[768]{0:T(1024)}, u32[]{:S(2)}) copy-start(f32[768]{0:T(1024)} %get-tuple-element.156) | copy-start | bytes 9220
  1457.7 605.3 %copy-start.62 = (f32[768]{0:T(1024)S(1)}, f32[768]{0:T(1024)}, u32[]{:S(2)}) copy-start(f32[768]{0:T(1024)} %get-tuple-element.161) | copy-start | bytes 9220
  1462.3 604.7 %copy-start.55 = (f32[9984]{0:T(1024)S(1)}, f32[9984]{0:T(1024)}, u32[]{:S(2)}) copy-start(f32[9984]{0:T(1024)} %param.40) | copy-start | bytes 119812
  1462.3 604.7 %copy-start.58 = (f32[9984]{0:T(1024)S(1)}, f32[9984]{0:T(1024)}, u32[]{:S(2)}) copy-start(f32[9984]{0:T(1024)} %param.41) | copy-start | bytes 119812
  2082.2 16.3 copy-start.28
  (60 other events, 326.2 us)
Sparse Core Ops, SparseCore 0:
  11.3 105.5 all-gather.1
  1440.4 9.5 reduce-scatter.4
  1452.8 11.9 reduce-scatter.2
